TPU v7x, 32 devices: a whole 2x2x4 slice. The times are simulated.
32 devices in a mesh: dp: 4 (over z), feat: 8 (over y, x, core).
Axes of the slice: x: 2, y: 2, z: 4, core: 2. Of those that a mesh axis runs over, the one named last changes fastest.
Arguments:
- clip_feats: bfloat16 [2, 384, 8192], P(None, 'dp', 'feat'), may hold values from 0 to 60
- proj_weight: bfloat16 [8192, 8192], P('dp', 'feat'), may hold values from -0.0625 to 0.0625
Outputs:
- loss_value: float32 [], replicated
- weight_grad: float32 [8192, 8192], P('dp', 'feat')
- redundancy: float32 [], replicated
- pair_similarity: float32 [384, 384], P('dp')
All inputs are finite; a program needn't handle non-finite values.
Results may differ from a plain program's by a relative error of at most 0.034.
Values may be sent and summed in bfloat16 or wider, within the bound.
A program may use at most 64 MiB of HBM per device.

v0:
```python
import math
import jax
import jax.numpy as jnp
from jax import lax
from jax.sharding import PartitionSpec as P

D = 8192
off_weight = 0.0051
epsilon = 1e-05
grad_scale = 32.0


def per_device(clip_feats, proj_weight):
    pairs = clip_feats.shape[1]
    width = clip_feats.shape[2]
    depth = proj_weight.shape[0]
    dp_count = lax.axis_size("dp")
    total = pairs * dp_count
    pair_count = float(total)
    gathered = lax.all_gather(clip_feats, "feat", axis=0, tiled=False)
    rows = lax.all_to_all(gathered, "dp", split_axis=0, concat_axis=0, tiled=True)
    parts = depth // width
    rows = rows.reshape(dp_count, parts, 2 * pairs, width).transpose(1, 0, 2, 3)
    rows = rows.reshape(parts, 2 * total, width)
    partial = sum(
        (
            jnp.dot(
                rows[i],
                proj_weight[i * width : (i + 1) * width],
                preferred_element_type=jnp.float32,
            )
            for i in range(parts)
        )
    ).reshape(dp_count, 2, pairs, width)
    partial = partial - jnp.mean(partial, axis=(0, 2), keepdims=True)
    columns = width // dp_count
    pieces = partial.astype(jnp.bfloat16).reshape(2 * total, width)
    pieces = jnp.stack([pieces[:, i * columns : (i + 1) * columns] for i in range(dp_count)])
    pieces = lax.all_to_all(pieces, "dp", split_axis=0, concat_axis=0, tiled=True)
    centered = jnp.sum(pieces.astype(jnp.float32), axis=0)
    centered = (
        centered.reshape(dp_count, 2, pairs, columns)
        .transpose(1, 0, 2, 3)
        .reshape(2, total, columns)
    )
    col_var = jnp.mean(centered * centered, axis=1, keepdims=True)
    col_scale = lax.rsqrt(col_var + epsilon)
    normed = centered * col_scale
    quantized = normed.astype(jnp.bfloat16)
    widened = quantized.astype(jnp.float32)
    gram_part = jnp.einsum("vpc,vnc->vpn", quantized, quantized, preferred_element_type=jnp.float32)
    diag_corr = jnp.sum(widened[0] * widened[1], axis=0) / pair_count
    diag_part = jnp.sum((1.0 - diag_corr) ** 2 - off_weight * diag_corr * diag_corr)
    square_part = jnp.sum(diag_corr * diag_corr)
    grams, diag_term, squares = lax.psum((gram_part, diag_part, square_part), ("dp", "feat"))
    frob_scaled = jnp.sum(grams[0] * grams[1]) / (pair_count * pair_count)
    loss_value = 16.0 * (diag_term + off_weight * frob_scaled) / float(D)
    redundancy = 8.0 * pair_count * (frob_scaled - squares) / (float(D) * float(D))
    first_row = lax.axis_index("dp") * pairs
    own = lax.dynamic_slice_in_dim(grams, first_row, pairs, axis=1)
    row_ids = lax.broadcasted_iota(jnp.int32, (pairs, total), 0) + first_row
    col_ids = lax.broadcasted_iota(jnp.int32, (pairs, total), 1)
    pair_similarity = jnp.where(
        row_ids == col_ids, 0.0, (own[0] + own[1]) / (2.0 * math.sqrt(float(D)))
    )
    slope = -2.0 * (1.0 - diag_corr) - 2.0 * off_weight * diag_corr
    coefficient = 2.0 * off_weight / (pair_count * pair_count)
    gram_q = grams.astype(jnp.bfloat16)
    cross_first = jnp.dot(gram_q[1], quantized[0], preferred_element_type=jnp.float32)
    cross_second = jnp.dot(gram_q[0], quantized[1], preferred_element_type=jnp.float32)
    grad_norm = jnp.stack(
        [
            slope * widened[1] / pair_count + coefficient * cross_first,
            slope * widened[0] / pair_count + coefficient * cross_second,
        ]
    )
    mean_one = jnp.mean(grad_norm, axis=1, keepdims=True)
    mean_two = jnp.mean(grad_norm * normed, axis=1, keepdims=True)
    pre_q = (col_scale * (grad_norm - mean_one - normed * mean_two)).astype(jnp.bfloat16)
    pre_q = (
        pre_q.reshape(2, dp_count, pairs, columns).transpose(1, 0, 2, 3).reshape(2 * total, columns)
    )
    flat_grad = lax.all_gather(pre_q, "dp", axis=1, tiled=True)
    summed = jnp.concatenate(
        [jnp.dot(rows[i].T, flat_grad, preferred_element_type=jnp.float32) for i in range(parts)]
    )
    return (loss_value, grad_scale * summed, redundancy, pair_similarity)


def solution(mesh):
    placed = (P(None, "dp", "feat"), P("dp", "feat"))
    return jax.shard_map(
        per_device,
        mesh=mesh,
        in_specs=placed,
        out_specs=(P(), P("dp", "feat"), P(), P("dp", None)),
        check_vma=False,
    )
```

profile of v0, /device:TPU:12, one launch (start us, length us, event | category | flops | bytes accessed | tf_op | source)
XLA Modules:
  0.0 368.9 jit_solution(855138404987530139)
XLA Ops:
  7.2 0.7 all-gather.6.cloned.1.call-update
  7.9 35.3 %all-gather.6.cloned.1.call-done = bf16[16,96,1024]{2,1,0:T(8,128)(2,1)} async-done(((bf16[2,96,1024]{2,1,0:T(8,128)(2,1)}), bf16[16,96,1024]{2,1,0:T(8,128)(2,1)}) %all-gather.6.cloned.1.call-update) | async-done | bytes 3145744 | tf_op jit(solution)/shard_map/all_gather | solution.py:20
  43.2 74.4 %all_to_all.10 = bf16[8,2,96,1024]{3,2,1,0:T(8,128)(2,1)S(1)} all-to-all(bf16[8,2,96,1024]{3,2,1,0:T(8,128)(2,1)} %bitcast.90), channel_id=1, replica_groups=mesh['dp'=4,'feat'=8] {'dp'}, dimensions={0} | all-to-all | bytes 6291456 | tf_op jit(solution)/shard_map/all_to_all | solution.py:21
  117.6 0.3 fusion.17
  118.0 3.0 copy-done.5
  120.9 1.8 fusion.1
  122.8 1.8 fusion.5
  124.6 0.2 reduce_sum.81
  124.8 0.4 fusion
  125.2 0.1 slice_bitcast_fusion.5
  125.3 0.2 pad_maximum_fusion
  125.6 39.1 %all_to_all.11 = bf16[4,768,256]{2,1,0:T(8,128)(2,1)S(1)} all-to-all(bf16[4,768,256]{2,1,0:T(8,128)(2,1)S(1)} %pad_maximum_fusion), channel_id=1, replica_groups=mesh['dp'=4,'feat'=8] {'dp'}, dimensions={0} | all-to-all | bytes 3145728 | tf_op jit(solution)/shard_map/all_to_all | solution.py:39
  164.7 0.2 convert_reduce_fusion
  164.9 0.1 multiply_reduce_fusion.1
  165.0 0.1 copy.9
  165.1 0.1 fusion.15
  165.2 1.4 fusion.18
  166.7 0.1 multiply_reduce_fusion.2
  166.7 0.6 multiply_reduce_fusion.3
  167.3 129.9 %all-reduce.3.cloned.1.call-done = f32[2,384,384]{2,1,0:T(8,128)} async-done(((f32[2,384,384]{2,1,0:T(8,128)}), f32[2,384,384]{2,1,0:T(8,128)}) %all-reduce.3.cloned.1.call-update) | async-done | bytes 1179664 | tf_op jit(solution)/shard_map/psum | solution.py:55
  297.2 1.3 convert_element_type.24
  298.6 0.3 fusion.9
  298.8 0.3 fusion.8
  299.1 0.1 maximum_reduce_fusion
  299.2 0.1 multiply_reduce_fusion
  299.3 0.9 multiply_convert_fusion
  300.3 46.0 %all-reduce = (f32[]{:T(128)}, f32[]{:T(128)}) all-reduce(f32[]{:T(128)} %get-tuple-element.5, f32[]{:T(128)} %get-tuple-element.4), channel_id=1, replica_groups=mesh['dp'=4,'feat'=8] {'dp','feat'}, use_global_device_ids=true, to_apply=%region_5.0 | all-reduce | flops 2 | bytes 16 | tf_op jit(solution)/shard_map/psum | solution.py:55
  346.3 0.7 fusion.11
  349.7 0.7 fusion.14
  350.4 3.4 convolution_bitcast_fusion
  353.8 1.8 convolution_bitcast_fusion.1
  355.7 4.4 %maximum_multiply_fusion = f32[2048,1024]{1,0:T(8,128)} fusion(f32[1024,1024]{1,0:T(8,128)S(1)} %convolution_bitcast_fusion, f32[1024,1024]{1,0:T(8,128)S(1)} %convolution_bitcast_fusion.1), kind=kLoop, calls=%fused_computation | loop fusion | flops 4194304 | bytes 16777216 | tf_op jit(solution)/shard_map/mul | solution.py:87
  (23 shorter events, 0.2 us)
Async XLA Ops:
  7.2 36.1 %all-gather.6.cloned.1.call-start = ((), (), s32[]{:S(2)}) async-start(), calls=%async_computation.4 | async-start | bytes 3538944 | tf_op jit(solution)/shard_map/all_gather | solution.py:20
  7.9 289.3 %all-reduce.3.cloned.1.call-start = ((), (), s32[]{:S(2)}) async-start(), calls=%async_computation.2 | async-start | bytes 2359296 | tf_op jit(solution)/shard_map/psum | solution.py:55
  117.6 3.3 copy-start.5
  117.9 4.8 %copy-start.3 = (bf16[1,4,192,1024]{3,2,0,1:T(8,128)(2,1)}, bf16[1,4,192,1024]{3,2,0,1:T(8,128)(2,1)S(1)}, u32[]{:S(2)}) copy-start(bf16[1,4,192,1024]{3,2,0,1:T(8,128)(2,1)S(1)} %get-tuple-element.11) | copy-start | bytes 4718596
  117.9 4.8 %copy-start.1 = (bf16[1,4,192,1024]{3,2,0,1:T(8,128)(2,1)}, bf16[1,4,192,1024]{3,2,0,1:T(8,128)(2,1)S(1)}, u32[]{:S(2)}) copy-start(bf16[1,4,192,1024]{3,2,0,1:T(8,128)(2,1)S(1)} %get-tuple-element.10) | copy-start | bytes 4718596
  166.6 183.8 %all-gather.4.cloned.1.call-start = ((), (), s32[]{:S(2)}) async-start(), calls=%async_computation.3 | async-start | bytes 1966080 | tf_op jit(solution)/shard_map/all_gather | solution.py:83
  299.3 47.0 %copy-start = (f32[2,384,384]{2,1,0:T(8,128)S(1)}, f32[2,384,384]{2,1,0:T(8,128)}, u32[]{:S(2)}) copy-start(f32[2,384,384]{2,1,0:T(8,128)} %all-reduce.3.cloned.1.call-done) | copy-start | bytes 3538948
  299.3 51.1 %copy-start.4 = (bf16[1,4,192,1024]{3,2,0,1:T(8,128)(2,1)S(1)}, bf16[1,4,192,1024]{3,2,0,1:T(8,128)(2,1)}, u32[]{:S(2)}) copy-start(bf16[1,4,192,1024]{3,2,0,1:T(8,128)(2,1)} %copy-done.3) | copy-start | bytes 4718596
  350.4 3.4 copy-start.2
  350.4 3.4 copy-start.6
Sparse Core Ops, SparseCore 0:
  9.9 33.3 all-gather.5
  166.7 130.4 all-reduce.2
  300.4 35.5 all-gather.3
where the time goes:
time: 369 us
  waiting for transfers between devices  166 us (45%)
  blocking collectives  160 us (43%)
  between operations  18.8 us (5%)
  matrix products  10.8 us (3%)
  other arithmetic  10.2 us (3%)
    psum x1, waiting for transfers between devices, per_device(): lax.psum((gram_part, diag_part, square_part), ('dp', 'feat'))  130 us
    all_to_all x1, blocking collectives, per_device(): lax.all_to_all(gathered, 'dp', split_axis=0, concat_axis=0, tiled=True)  74.4 us
    psum x1, blocking collectives, per_device(): lax.psum((gram_part, diag_part, square_part), ('dp', 'feat'))  46 us
    all_to_all x1, blocking collectives, per_device(): lax.all_to_all(pieces, 'dp', split_axis=0, concat_axis=0, tiled=True)  39.1 us
    all_gather x1, waiting for transfers between devices, per_device(): gathered = lax.all_gather(clip_feats, 'feat', axis=0, tiled=False)  35.3 us
  transfers between devices with their start and end apart: 3, of which 2 were waited for; matrix products, arithmetic and copies ran while one was open for 1% of the time, Pallas kernels for 0%

commit v1 on v0

--- a/solution.py
+++ b/solution.py
@@ -52,7 +52,13 @@
     diag_corr = jnp.sum(widened[0] * widened[1], axis=0) / pair_count
     diag_part = jnp.sum((1.0 - diag_corr) ** 2 - off_weight * diag_corr * diag_corr)
     square_part = jnp.sum(diag_corr * diag_corr)
-    grams, diag_term, squares = lax.psum((gram_part, diag_part, square_part), ("dp", "feat"))
+
+    def close_rails(in_array):
+        for k0 in ("feat", "dp"):
+            in_array = lax.psum(in_array, axis_name=k0)
+        return in_array
+
+    grams, diag_term, squares = close_rails((gram_part, diag_part, square_part))
     frob_scaled = jnp.sum(grams[0] * grams[1]) / (pair_count * pair_count)
     loss_value = 16.0 * (diag_term + off_weight * frob_scaled) / float(D)
     redundancy = 8.0 * pair_count * (frob_scaled - squares) / (float(D) * float(D))

time: 369 us -> 342 us (0.927); the launches traced: 369 us -> 338 us
  blocking collectives: 160 us -> 137 us
  waiting for transfers between devices: 166 us -> 158 us
    psum x1 -> x2, blocking collectives: 46 us -> 23.2 us  [close_rails(): in_array = lax.psum(in_array, axis_name=k0)]
    psum x1 -> x2, waiting for transfers between devices: 130 us -> 113 us  [close_rails(): in_array = lax.psum(in_array, axis_name=k0)]
    all_gather x1, waiting for transfers between devices: 0.01 us -> 8.25 us  [per_device(): flat_grad = lax.all_gather(pre_q, 'dp', axis=1, tiled=True)]
  transfers between devices with their start and end apart: 3 -> 4, of which waited for: 2 -> 4; matrix products, arithmetic and copies ran while one was open for 1% -> 1% of each run, Pallas kernels for 0% -> 0%
where the time goes in v1:
time: 342 us; the launch traced here: 338 us
  waiting for transfers between devices  158 us (46%)
  blocking collectives  137 us (40%)
  between operations  18.8 us (5%)
  matrix products  10.8 us (3%)
  other arithmetic  10.2 us (3%)
  local copies, waits for them, and re-layouts  3.5 us (1%)
    psum x2, waiting for transfers between devices, close_rails(): in_array = lax.psum(in_array, axis_name=k0)  113 us
    all_to_all x1, blocking collectives, per_device(): lax.all_to_all(gathered, 'dp', split_axis=0, concat_axis=0, tiled=True)  74.4 us
    all_to_all x1, blocking collectives, per_device(): lax.all_to_all(pieces, 'dp', split_axis=0, concat_axis=0, tiled=True)  39.1 us
    all_gather x1, waiting for transfers between devices, per_device(): gathered = lax.all_gather(clip_feats, 'feat', axis=0, tiled=False)  35.3 us
    psum x2, blocking collectives, close_rails(): in_array = lax.psum(in_array, axis_name=k0)  23.2 us
    all_gather x1, waiting for transfers between devices, per_device(): flat_grad = lax.all_gather(pre_q, 'dp', axis=1, tiled=True)  8.25 us
  transfers between devices with their start and end apart: 4, of which 4 were waited for; matrix products, arithmetic and copies ran while one was open for 1% of the time, Pallas kernels for 0%

profile of v1, /device:TPU:12, one launch (start us, length us, event | category | flops | bytes accessed | tf_op | source)
XLA Modules:
  0.0 338.0 jit_solution(8771795915944411042)
XLA Ops:
  7.2 0.7 all-gather.6.cloned.1.call-update
  7.9 35.3 %all-gather.6.cloned.1.call-done = bf16[16,96,1024]{2,1,0:T(8,128)(2,1)} async-done(((bf16[2,96,1024]{2,1,0:T(8,128)(2,1)}), bf16[16,96,1024]{2,1,0:T(8,128)(2,1)}) %all-gather.6.cloned.1.call-update) | async-done | bytes 3145744 | tf_op jit(solution)/shard_map/all_gather | solution.py:20
  43.2 74.4 %all_to_all.10 = bf16[8,2,96,1024]{3,2,1,0:T(8,128)(2,1)S(1)} all-to-all(bf16[8,2,96,1024]{3,2,1,0:T(8,128)(2,1)} %bitcast.90), channel_id=1, replica_groups=mesh['dp'=4,'feat'=8] {'dp'}, dimensions={0} | all-to-all | bytes 6291456 | tf_op jit(solution)/shard_map/all_to_all | solution.py:21
  117.6 0.3 fusion.17
  118.0 3.0 copy-done.5
  120.9 1.8 fusion.1
  122.8 1.8 fusion.5
  124.6 0.2 reduce_sum.81
  124.8 0.4 fusion
  125.2 0.1 slice_bitcast_fusion.5
  125.3 0.2 pad_maximum_fusion
  125.6 39.1 %all_to_all.11 = bf16[4,768,256]{2,1,0:T(8,128)(2,1)S(1)} all-to-all(bf16[4,768,256]{2,1,0:T(8,128)(2,1)S(1)} %pad_maximum_fusion), channel_id=1, replica_groups=mesh['dp'=4,'feat'=8] {'dp'}, dimensions={0} | all-to-all | bytes 3145728 | tf_op jit(solution)/shard_map/all_to_all | solution.py:39
  164.7 0.2 convert_reduce_fusion
  164.9 0.1 multiply_reduce_fusion.1
  165.1 0.1 fusion.15
  165.2 1.4 fusion.18
  166.7 55.8 %all-reduce.5.cloned.1.call-done = f32[2,384,384]{2,1,0:T(8,128)} async-done(((f32[2,384,384]{2,1,0:T(8,128)}), f32[2,384,384]{2,1,0:T(8,128)}) %all-reduce.5.cloned.1.call-update) | async-done | bytes 1179664 | tf_op jit(solution)/shard_map/psum | solution.py:58
  222.7 0.6 multiply_reduce_fusion.3
  223.3 57.6 %all-reduce.7.cloned.1.call-done = f32[2,384,384]{2,1,0:T(8,128)} async-done(((f32[2,384,384]{2,1,0:T(8,128)}), f32[2,384,384]{2,1,0:T(8,128)}) %all-reduce.7.cloned.1.call-update) | async-done | bytes 1179664 | tf_op jit(solution)/shard_map/psum | solution.py:58
  280.9 1.3 convert_element_type.24
  282.2 0.3 fusion.9
  282.5 0.3 fusion.8
  282.9 0.1 multiply_reduce_fusion
  283.0 0.9 multiply_convert_fusion
  284.0 13.1 %all-reduce = (f32[]{:T(128)}, f32[]{:T(128)}) all-reduce(f32[]{:T(128)} %get-tuple-element.5, f32[]{:T(128)} %get-tuple-element.4), channel_id=1, replica_groups=mesh['dp'=4,'feat'=8] {'feat'}, use_global_device_ids=true, to_apply=%region_5.0 | all-reduce | flops 2 | bytes 16 | tf_op jit(solution)/shard_map/psum | solution.py:58
  297.1 10.1 %all-reduce.1 = (f32[]{:T(128)}, f32[]{:T(128)}) all-reduce(f32[]{:T(128)} %get-tuple-element.6, f32[]{:T(128)} %get-tuple-element.7), channel_id=1, replica_groups=mesh['dp'=4,'feat'=8] {'dp'}, use_global_device_ids=true, to_apply=%region_6.0 | all-reduce | flops 2 | bytes 16 | tf_op jit(solution)/shard_map/psum | solution.py:58
  307.2 0.7 fusion.11
  310.5 0.7 fusion.14
  311.3 8.3 %all-gather.4.cloned.1.call-done = bf16[768,1024]{1,0:T(8,128)(2,1)} async-done(((bf16[768,256]{1,0:T(8,128)(2,1)}), bf16[768,1024]{1,0:T(8,128)(2,1)}) %all-gather.4.cloned.1.call-update) | async-done | bytes 1572880 | tf_op jit(solution)/shard_map/all_gather | solution.py:89
  319.6 3.4 %convolution_bitcast_fusion = f32[1024,1024]{1,0:T(8,128)S(1)} fusion(bf16[768,1024]{1,0:T(8,128)(2,1)} %all-gather.4.cloned.1.call-done, bf16[768,1024]{1,0:T(8,128)(2,1)S(1)} %bitcast.95), kind=kOutput, calls=%fused_computation.4 | convolution fusion | flops 1610612736 | bytes 7340032 | tf_op jit(solution)/shard_map/dot_general | solution.py:91
  323.0 1.8 convolution_bitcast_fusion.1
  324.8 4.4 %maximum_multiply_fusion = f32[2048,1024]{1,0:T(8,128)} fusion(f32[1024,1024]{1,0:T(8,128)S(1)} %convolution_bitcast_fusion, f32[1024,1024]{1,0:T(8,128)S(1)} %convolution_bitcast_fusion.1), kind=kLoop, calls=%fused_computation | loop fusion | flops 4194304 | bytes 16777216 | tf_op jit(solution)/shard_map/mul | solution.py:93
  (27 shorter events, 0.5 us)
Async XLA Ops:
  7.2 36.1 %all-gather.6.cloned.1.call-start = ((), (), s32[]{:S(2)}) async-start(), calls=%async_computation.5 | async-start | bytes 3538944 | tf_op jit(solution)/shard_map/all_gather | solution.py:20
  7.9 214.6 %all-reduce.5.cloned.1.call-start = ((), (), s32[]{:S(2)}) async-start(), calls=%async_computation.2 | async-start | bytes 2359296 | tf_op jit(solution)/shard_map/psum | solution.py:58
  117.6 3.3 copy-start.5
  117.9 4.8 %copy-start.3 = (bf16[1,4,192,1024]{3,2,0,1:T(8,128)(2,1)}, bf16[1,4,192,1024]{3,2,0,1:T(8,128)(2,1)S(1)}, u32[]{:S(2)}) copy-start(bf16[1,4,192,1024]{3,2,0,1:T(8,128)(2,1)S(1)} %get-tuple-element.13) | copy-start | bytes 4718596
  117.9 4.8 %copy-start.1 = (bf16[1,4,192,1024]{3,2,0,1:T(8,128)(2,1)}, bf16[1,4,192,1024]{3,2,0,1:T(8,128)(2,1)S(1)}, u32[]{:S(2)}) copy-start(bf16[1,4,192,1024]{3,2,0,1:T(8,128)(2,1)S(1)} %get-tuple-element.12) | copy-start | bytes 4718596
  166.6 114.3 %all-reduce.7.cloned.1.call-start = ((), (), s32[]{:S(2)}) async-start(), calls=%async_computation.3 | async-start | bytes 2359296 | tf_op jit(solution)/shard_map/psum | solution.py:58
  222.5 97.0 %all-gather.4.cloned.1.call-start = ((), (), s32[]{:S(2)}) async-start(), calls=%async_computation.4 | async-start | bytes 1966080 | tf_op jit(solution)/shard_map/all_gather | solution.py:89
  283.0 24.2 %copy-start = (f32[2,384,384]{2,1,0:T(8,128)S(1)}, f32[2,384,384]{2,1,0:T(8,128)}, u32[]{:S(2)}) copy-start(f32[2,384,384]{2,1,0:T(8,128)} %all-reduce.7.cloned.1.call-done) | copy-start | bytes 3538948
  283.0 36.6 %copy-start.4 = (bf16[1,4,192,1024]{3,2,0,1:T(8,128)(2,1)S(1)}, bf16[1,4,192,1024]{3,2,0,1:T(8,128)(2,1)}, u32[]{:S(2)}) copy-start(bf16[1,4,192,1024]{3,2,0,1:T(8,128)(2,1)} %copy-done.3) | copy-start | bytes 4718596
  311.3 11.7 %copy-start.2 = (bf16[1,4,192,1024]{3,2,0,1:T(8,128)(2,1)S(1)}, bf16[1,4,192,1024]{3,2,0,1:T(8,128)(2,1)}, u32[]{:S(2)}) copy-start(bf16[1,4,192,1024]{3,2,0,1:T(8,128)(2,1)} %copy-done.1) | copy-start | bytes 4718596
  319.6 3.4 %copy-start.6 = (bf16[768,1024]{1,0:T(8,128)(2,1)S(1)}, bf16[768,1024]{1,0:T(8,128)(2,1)}, u32[]{:S(2)}) copy-start(bf16[768,1024]{1,0:T(8,128)(2,1)} %all-gather.4.cloned.1.call-done) | copy-start | bytes 4718596
Sparse Core Ops, SparseCore 0:
  9.9 33.3 all-gather.5
  166.7 55.7 all-reduce.4
  225.0 55.8 all-reduce.6
  284.1 35.4 all-gather.3
